TPU v7x, 128 devices: a whole 4x4x4 slice. The times are simulated.
128 devices in a mesh: gz: 16 (over x, y_lo, core), gy: 8 (over y_hi, z).
Axes of the slice: x: 4, y: 4 (y_hi: 2, y_lo: 2; y = y_hi * 2 + y_lo), z: 4, core: 2. Of those that a mesh axis runs over, the one named last changes fastest.
Arguments:
- e_field: float32 [3, 512, 128, 256], P(None, 'gz', 'gy'), may hold values from -6 to 6
- h_field: float32 [3, 512, 128, 256], P(None, 'gz', 'gy'), may hold values from -6 to 6
- e_coef: float32 [512, 128, 256], P('gz', 'gy'), may hold values from 0.14 to 0.55
- e_loss: float32 [512, 128, 256], P('gz', 'gy'), may hold values from 0 to 0.1
- port_cell: int32 [4096], P(('gz', 'gy')), may hold values from 0 to 131071
- port_node: int32 [4096], replicated, may hold values from 0 to 16383
- port_gain: float32 [4096], replicated, may hold values from 0.5 to 2
- diag_blocks: float32 [256, 64, 64], P(('gz', 'gy')), may hold values from -0.5 to 4.5, as said below
- inv_blocks: float32 [256, 64, 64], P(('gz', 'gy')), may hold values from -0.012 to 0.247, as said below
- off_blocks: float32 [256, 4, 64, 64], P(('gz', 'gy')), may hold values from -0.1875 to 0.1875
- off_cols: int32 [256, 4], P(('gz', 'gy')), may hold values from 0 to 255
- volts_init: float32 [16384], P(('gz', 'gy')), may hold values from -6 to 6
Outputs:
- e_final: float32 [3, 512, 128, 256], P(None, 'gz', 'gy')
- h_final: float32 [3, 512, 128, 256], P(None, 'gz', 'gy')
- node_volts: float32 [16384], P(('gz', 'gy'))
Inputs may be any that keep to these rules, and one draw needn't show every extreme that they name: `diag_blocks`: 4 times the identity plus independent entries of spread 1/8. `inv_blocks`: 0.235 times the identity plus small independent entries. `port_cell`: ports may share a cell.
All inputs are finite; a program needn't handle non-finite values.
Results may differ from a plain program's by a relative error of at most 0.00019.
Values sent between devices are 32-bit elements; how exact they have to be, the bound alone decides.
No kernel may reach another device: no remote copies, remote signals or barrier semaphores. Data moves between devices by JAX's collectives and lax.ppermute only.
A program may use at most 64 MiB of HBM per device.

v0:
```python
import jax
import jax.numpy as jnp
from jax import lax
from jax.sharding import PartitionSpec as P

STEPS = 5
NEWTON = 2
BS = 64
NB_DEV = 2
PORT_DEV = 32
precise = lax.Precision.HIGHEST
time_step = 0.55
charge_scale = 4.0
diode_weight = 0.5


def shifted(value, axis, steps):
    count = lax.axis_size(axis)
    first, last = (max(0, -steps), min(count, count - steps))
    return lax.ppermute(value, axis, [(source, source + steps) for source in range(first, last)])


def update_magnetic(e_now, h_now):
    upper_z = shifted(e_now[0:2, 0], "gz", -1)
    upper_y = shifted(jnp.stack([e_now[0, :, 0], e_now[2, :, 0]]), "gy", -1)
    above_z = jnp.concatenate([e_now[0:2, 1:], upper_z[:, None]], axis=1)
    inner_y = jnp.stack([e_now[0, :, 1:], e_now[2, :, 1:]])
    above_y = jnp.concatenate([inner_y, upper_y[:, :, None]], axis=2)
    blank = jnp.zeros((2,) + e_now.shape[1:3] + (1,), jnp.float32)
    above_x = jnp.concatenate([e_now[1:3, :, :, 1:], blank], axis=3)
    curl_x = above_y[1] - e_now[2] - (above_z[1] - e_now[1])
    curl_y = above_z[0] - e_now[0] - (above_x[1] - e_now[2])
    curl_z = above_x[0] - e_now[1] - (above_y[0] - e_now[0])
    return h_now - time_step * jnp.stack([curl_x, curl_y, curl_z])


def update_electric(e_now, h_now, e_coef, e_loss):
    lower_z = shifted(h_now[0:2, -1], "gz", 1)
    lower_y = shifted(jnp.stack([h_now[0, :, -1], h_now[2, :, -1]]), "gy", 1)
    below_z = jnp.concatenate([lower_z[:, None], h_now[0:2, :-1]], axis=1)
    inner_y = jnp.stack([h_now[0, :, :-1], h_now[2, :, :-1]])
    below_y = jnp.concatenate([lower_y[:, :, None], inner_y], axis=2)
    blank = jnp.zeros((2,) + h_now.shape[1:3] + (1,), jnp.float32)
    below_x = jnp.concatenate([blank, h_now[1:3, :, :, :-1]], axis=3)
    back_x = h_now[2] - below_y[1] - (h_now[1] - below_z[1])
    back_y = h_now[0] - below_z[0] - (h_now[2] - below_x[1])
    back_z = h_now[1] - below_x[0] - (h_now[0] - below_y[0])
    return (1.0 - e_loss) * e_now + e_coef * jnp.stack([back_x, back_y, back_z])


def whole_terms(
    volts_all, samples_all, port_node, port_gain, off_blocks, off_cols, own_nodes, first_node
):
    blocks_all = volts_all.reshape(-1, BS)
    picked = blocks_all[off_cols]
    offsum = jnp.einsum("jkab,jkb->ja", off_blocks, picked, precision=precise)
    columns = jnp.arange(NB_DEV * BS, dtype=jnp.int32)
    onehot = ((port_node - first_node)[:, None] == columns[None, :]).astype(jnp.float32)
    inject = jnp.dot(port_gain * samples_all, onehot, precision=precise).reshape(NB_DEV, BS)
    near = volts_all[own_nodes]
    return (offsum, inject, near)


def newton_solve(volts, offsum, inject, diag_blocks, inv_blocks):
    vstart = volts.reshape(NB_DEV, BS)
    target = charge_scale * vstart + inject - offsum
    iterate = vstart
    for newton_round in range(NEWTON):
        resid = (
            jnp.einsum("jab,jb->ja", diag_blocks, iterate, precision=precise)
            + diode_weight * jnp.tanh(iterate)
            - target
        )
        iterate = iterate - jnp.einsum("jab,jb->ja", inv_blocks, resid, precision=precise)
    return iterate.reshape(-1)


def body(
    e_field,
    h_field,
    e_coef,
    e_loss,
    port_cell,
    port_node,
    port_gain,
    diag_blocks,
    inv_blocks,
    off_blocks,
    off_cols,
    volts_init,
):
    device = lax.axis_index(("gz", "gy"))
    first_node = device * (NB_DEV * BS)
    own_nodes = lax.dynamic_slice_in_dim(port_node, device * PORT_DEV, PORT_DEV)
    own_gain = lax.dynamic_slice_in_dim(port_gain, device * PORT_DEV, PORT_DEV)
    coef_flat = e_coef.reshape(-1)
    cell_coef = coef_flat[port_cell]
    depth, height, width = e_coef.shape

    def circuit_inputs(volts, samples):
        volts_all, samples_all = (
            lax.all_gather(volts, ("gz", "gy"), axis=0, tiled=True),
            lax.all_gather(samples, ("gz", "gy"), axis=0, tiled=True),
        )
        return whole_terms(
            volts_all,
            samples_all,
            port_node,
            port_gain,
            off_blocks,
            off_cols,
            own_nodes,
            first_node,
        )

    def advance(step_index, state):
        e_now, h_now, volts, samples = state
        offsum, inject, near = circuit_inputs(volts, samples)
        h_new = update_magnetic(e_now, h_now)
        e_new = update_electric(e_now, h_new, e_coef, e_loss)
        current = own_gain * (samples - near)
        new_z = e_new[2].reshape(-1).at[port_cell].add(-cell_coef * current)
        e_new = jnp.stack([e_new[0], e_new[1], new_z.reshape(depth, height, width)])
        volts_new = newton_solve(volts, offsum, inject, diag_blocks, inv_blocks)
        samples_new = e_new[2].reshape(-1)[port_cell]
        return (e_new, h_new, volts_new, samples_new)

    samples_start = e_field[2].reshape(-1)[port_cell]
    e_end, h_end, volts_end, samples_end = lax.fori_loop(
        0, STEPS, advance, (e_field, h_field, volts_init, samples_start)
    )
    return (e_end, h_end, volts_end)


def solution(mesh):
    placed = (
        P(None, "gz", "gy", None),
        P(None, "gz", "gy", None),
        P("gz", "gy", None),
        P("gz", "gy", None),
        P(("gz", "gy")),
        P(),
        P(),
        P(("gz", "gy"), None, None),
        P(("gz", "gy"), None, None),
        P(("gz", "gy"), None, None, None),
        P(("gz", "gy"), None),
        P(("gz", "gy")),
    )
    return jax.shard_map(
        body,
        mesh=mesh,
        in_specs=placed,
        out_specs=(P(None, "gz", "gy", None), P(None, "gz", "gy", None), P(("gz", "gy"))),
        check_vma=False,
    )
```

profile of v0, /device:TPU:16, one launch (start us, length us, event | category | flops | bytes accessed | tf_op | source)
XLA Modules:
  0.0 2143.5 jit_solution(3278946582006856271)
XLA Ops:
  4.6 2.1 gather_fusion.3
  6.8 2.1 copy.48
  8.9 1.6 gather_fusion.4
  11.0 2130.8 %while.18 = (s32[]{:T(128)}, f32[3,32,16,256]{3,2,1,0:T(8,128)S(1)}, f32[3,32,16,256]{3,2,1,0:T(8,128)S(1)}, f32[128]{0:T(128)S(1)}, f32[32]{0:T(128)}, /*index=...) while((s32[]{:T(128)}, ...), condition=%wide.region_2.0_spmd, body=%wide.region_0.0_spmd.sunk | while | flops 15647837 | bytes 67082616 | solution.py:129
  12.6 5.7 collective-permute-start.1
  25.0 1.9 broadcast_subtract_fusion.4
  26.9 306.8 %all-gather.2 = f32[128,1,128]{2,1,0:T(1,128)S(1)} all-gather(f32[1,1,128]{2,1,0:T(1,128)S(1)} %bitcast.168), channel_id=1, replica_groups=mesh['gz'=16,'gy'=8] {'gz','gy'}, dimensions={0}, use_global_device_ids=true | all-gather | bytes 66048 | tf_op jit(solution)/shard_map/while/body/eval_jaxpr/all_gather | solution.py:102
  338.6 69.4 %all-reduce.4 = f32[4096]{0:T(1024)S(1)} all-reduce(f32[4096]{0:T(1024)S(1)} %dynamic-update-slice.2), channel_id=1, replica_groups=mesh['gz'=16,'gy'=8] {'gz','gy'}, use_global_device_ids=true, to_apply=%add.2 | all-reduce | flops 4096 | bytes 32768 | tf_op jit(solution)/shard_map/while
  409.8 1.5 gather_fusion.1
  424.5 1.9 collective-permute-start.3
  426.6 1.6 collective-permute-start.2
  428.2 6.0 collective-permute-done.3
  440.9 1.5 pad_maximum_fusion.13
  444.0 1.9 collective-permute-start.1
  452.6 1.9 broadcast_subtract_fusion.4
  454.5 304.1 %all-gather.2 = f32[128,1,128]{2,1,0:T(1,128)S(1)} all-gather(f32[1,1,128]{2,1,0:T(1,128)S(1)} %bitcast.168), channel_id=1, replica_groups=mesh['gz'=16,'gy'=8] {'gz','gy'}, dimensions={0}, use_global_device_ids=true | all-gather | bytes 66048 | tf_op jit(solution)/shard_map/while/body/eval_jaxpr/all_gather | solution.py:102
  763.4 69.4 %all-reduce.4 = f32[4096]{0:T(1024)S(1)} all-reduce(f32[4096]{0:T(1024)S(1)} %dynamic-update-slice.2), channel_id=1, replica_groups=mesh['gz'=16,'gy'=8] {'gz','gy'}, use_global_device_ids=true, to_apply=%add.2 | all-reduce | flops 4096 | bytes 32768 | tf_op jit(solution)/shard_map/while
  834.6 1.5 gather_fusion.1
  849.3 1.9 collective-permute-start.3
  851.4 1.6 collective-permute-start.2
  853.1 6.0 collective-permute-done.3
  865.7 1.5 pad_maximum_fusion.13
  868.9 1.9 collective-permute-start.1
  877.4 1.9 broadcast_subtract_fusion.4
  879.3 304.1 %all-gather.2 = f32[128,1,128]{2,1,0:T(1,128)S(1)} all-gather(f32[1,1,128]{2,1,0:T(1,128)S(1)} %bitcast.168), channel_id=1, replica_groups=mesh['gz'=16,'gy'=8] {'gz','gy'}, dimensions={0}, use_global_device_ids=true | all-gather | bytes 66048 | tf_op jit(solution)/shard_map/while/body/eval_jaxpr/all_gather | solution.py:102
  1188.3 69.4 %all-reduce.4 = f32[4096]{0:T(1024)S(1)} all-reduce(f32[4096]{0:T(1024)S(1)} %dynamic-update-slice.2), channel_id=1, replica_groups=mesh['gz'=16,'gy'=8] {'gz','gy'}, use_global_device_ids=true, to_apply=%add.2 | all-reduce | flops 4096 | bytes 32768 | tf_op jit(solution)/shard_map/while
  1274.2 1.9 collective-permute-start.3
  1276.3 1.6 collective-permute-start.2
  1277.9 6.0 collective-permute-done.3
  1290.6 1.5 pad_maximum_fusion.13
  1293.7 1.9 collective-permute-start.1
  1302.3 1.9 broadcast_subtract_fusion.4
  1304.2 304.1 %all-gather.2 = f32[128,1,128]{2,1,0:T(1,128)S(1)} all-gather(f32[1,1,128]{2,1,0:T(1,128)S(1)} %bitcast.168), channel_id=1, replica_groups=mesh['gz'=16,'gy'=8] {'gz','gy'}, dimensions={0}, use_global_device_ids=true | all-gather | bytes 66048 | tf_op jit(solution)/shard_map/while/body/eval_jaxpr/all_gather | solution.py:102
  1613.1 69.4 %all-reduce.4 = f32[4096]{0:T(1024)S(1)} all-reduce(f32[4096]{0:T(1024)S(1)} %dynamic-update-slice.2), channel_id=1, replica_groups=mesh['gz'=16,'gy'=8] {'gz','gy'}, use_global_device_ids=true, to_apply=%add.2 | all-reduce | flops 4096 | bytes 32768 | tf_op jit(solution)/shard_map/while
  1684.3 1.5 gather_fusion.1
  1699.0 1.9 collective-permute-start.3
  1701.1 1.6 collective-permute-start.2
  1702.8 6.0 collective-permute-done.3
  1715.4 1.5 pad_maximum_fusion.13
  1718.6 1.9 collective-permute-start.1
  1727.1 1.9 broadcast_subtract_fusion.4
  1729.0 304.1 %all-gather.2 = f32[128,1,128]{2,1,0:T(1,128)S(1)} all-gather(f32[1,1,128]{2,1,0:T(1,128)S(1)} %bitcast.168), channel_id=1, replica_groups=mesh['gz'=16,'gy'=8] {'gz','gy'}, dimensions={0}, use_global_device_ids=true | all-gather | bytes 66048 | tf_op jit(solution)/shard_map/while/body/eval_jaxpr/all_gather | solution.py:102
  2038.0 69.4 %all-reduce.4 = f32[4096]{0:T(1024)S(1)} all-reduce(f32[4096]{0:T(1024)S(1)} %dynamic-update-slice.2), channel_id=1, replica_groups=mesh['gz'=16,'gy'=8] {'gz','gy'}, use_global_device_ids=true, to_apply=%add.2 | all-reduce | flops 4096 | bytes 32768 | tf_op jit(solution)/shard_map/while
  2109.2 1.5 gather_fusion.1
  2123.9 1.9 collective-permute-start.3
  2126.0 1.6 collective-permute-start.2
  2127.6 6.0 collective-permute-done.3
  2140.3 1.5 pad_maximum_fusion.13
  (470 shorter events, 180.7 us)
Async XLA Ops:
  3.5 7.5 copy-start.2
  3.5 7.5 copy-start.7
  3.6 7.5 copy-start.15
  11.0 322.7 %copy-start.20 = (s32[32]{0:T(128)}, s32[32]{0:T(128)S(1)}, u32[]{:S(2)}) copy-start(s32[32]{0:T(128)S(1)} %get-tuple-element.465) | copy-start | bytes 388 | tf_op jit(solution)/shard_map/while
  12.6 407.6 %collective-permute-start.1 = (f32[2,32,256]{2,1,0:T(8,128)}, f32[2,32,256]{2,1,0:T(8,128)}, u32[]{:S(2)}, u32[]{:S(2)}) collective-permute-start(f32[2,32,256]{2,1,0:T(8,128)} %pad_maximum_fusion.10), channel_id=1, source_target_pairs={{1,0},{2,1},{3,2},{4,3},{5,4},{6,5},{7,6},{9,8},{10,9},{11,10},{12... | collective-permute-start | bytes 196616 | tf_op jit(solution)/shard_map/while/body/eval_jaxpr/ppermute | solution.py:20
  19.0 403.5 %collective-permute-start = (f32[2,16,256]{2,1,0:T(8,128)}, f32[2,16,256]{2,1,0:T(8,128)}, u32[]{:S(2)}, u32[]{:S(2)}) collective-permute-start(f32[2,16,256]{2,1,0:T(8,128)} %slice_bitcast_fusion.7), channel_id=1, source_target_pairs={{8,0},{16,8},{24,16},{32,24},{40,32},{48,40},{56,48},{64,56},{72,6... | collective-permute-start | bytes 98312 | tf_op jit(solution)/shard_map/while/body/eval_jaxpr/ppermute | solution.py:20
  337.0 82.1 %copy-start.12 = (f32[32]{0:T(128)S(1)}, f32[32]{0:T(128)}, u32[]{:S(2)}) copy-start(f32[32]{0:T(128)} %get-tuple-element.438) | copy-start | bytes 388 | tf_op jit(solution)/shard_map/while
  337.0 82.1 %copy-start.16 = (f32[32]{0:T(128)S(1)}, f32[32]{0:T(128)}, u32[]{:S(2)}) copy-start(f32[32]{0:T(128)} %get-tuple-element.466) | copy-start | bytes 388 | tf_op jit(solution)/shard_map/while
  337.0 82.1 %copy-start.17 = (f32[32]{0:T(128)S(1)}, f32[32]{0:T(128)}, u32[]{:S(2)}) copy-start(f32[32]{0:T(128)} %get-tuple-element.467) | copy-start | bytes 388 | tf_op jit(solution)/shard_map/while
  337.0 82.7 %copy-start.9 = (s32[32]{0:T(128)S(1)}, s32[32]{0:T(128)}, u32[]{:S(2)}) copy-start(s32[32]{0:T(128)} %get-tuple-element.409) | copy-start | bytes 388 | tf_op jit(solution)/shard_map/while
  424.5 9.8 collective-permute-start.3
  426.6 7.9 collective-permute-start.2
  442.4 316.1 %copy-start.20 = (s32[32]{0:T(128)}, s32[32]{0:T(128)S(1)}, u32[]{:S(2)}) copy-start(s32[32]{0:T(128)S(1)} %get-tuple-element.465) | copy-start | bytes 388 | tf_op jit(solution)/shard_map/while
  444.0 401.1 %collective-permute-start.1 = (f32[2,32,256]{2,1,0:T(8,128)}, f32[2,32,256]{2,1,0:T(8,128)}, u32[]{:S(2)}, u32[]{:S(2)}) collective-permute-start(f32[2,32,256]{2,1,0:T(8,128)} %pad_maximum_fusion.10), channel_id=1, source_target_pairs={{1,0},{2,1},{3,2},{4,3},{5,4},{6,5},{7,6},{9,8},{10,9},{11,10},{12... | collective-permute-start | bytes 196616 | tf_op jit(solution)/shard_map/while/body/eval_jaxpr/ppermute | solution.py:20
  446.5 400.8 %collective-permute-start = (f32[2,16,256]{2,1,0:T(8,128)}, f32[2,16,256]{2,1,0:T(8,128)}, u32[]{:S(2)}, u32[]{:S(2)}) collective-permute-start(f32[2,16,256]{2,1,0:T(8,128)} %slice_bitcast_fusion.7), channel_id=1, source_target_pairs={{8,0},{16,8},{24,16},{32,24},{40,32},{48,40},{56,48},{64,56},{72,6... | collective-permute-start | bytes 98312 | tf_op jit(solution)/shard_map/while/body/eval_jaxpr/ppermute | solution.py:20
  761.8 82.1 %copy-start.12 = (f32[32]{0:T(128)S(1)}, f32[32]{0:T(128)}, u32[]{:S(2)}) copy-start(f32[32]{0:T(128)} %get-tuple-element.438) | copy-start | bytes 388 | tf_op jit(solution)/shard_map/while
  761.8 82.1 %copy-start.16 = (f32[32]{0:T(128)S(1)}, f32[32]{0:T(128)}, u32[]{:S(2)}) copy-start(f32[32]{0:T(128)} %get-tuple-element.466) | copy-start | bytes 388 | tf_op jit(solution)/shard_map/while
  761.8 82.1 %copy-start.17 = (f32[32]{0:T(128)S(1)}, f32[32]{0:T(128)}, u32[]{:S(2)}) copy-start(f32[32]{0:T(128)} %get-tuple-element.467) | copy-start | bytes 388 | tf_op jit(solution)/shard_map/while
  761.8 82.7 %copy-start.9 = (s32[32]{0:T(128)S(1)}, s32[32]{0:T(128)}, u32[]{:S(2)}) copy-start(s32[32]{0:T(128)} %get-tuple-element.409) | copy-start | bytes 388 | tf_op jit(solution)/shard_map/while
  849.3 9.8 collective-permute-start.3
  851.4 7.9 collective-permute-start.2
  867.3 316.1 %copy-start.20 = (s32[32]{0:T(128)}, s32[32]{0:T(128)S(1)}, u32[]{:S(2)}) copy-start(s32[32]{0:T(128)S(1)} %get-tuple-element.465) | copy-start | bytes 388 | tf_op jit(solution)/shard_map/while
  868.9 401.1 %collective-permute-start.1 = (f32[2,32,256]{2,1,0:T(8,128)}, f32[2,32,256]{2,1,0:T(8,128)}, u32[]{:S(2)}, u32[]{:S(2)}) collective-permute-start(f32[2,32,256]{2,1,0:T(8,128)} %pad_maximum_fusion.10), channel_id=1, source_target_pairs={{1,0},{2,1},{3,2},{4,3},{5,4},{6,5},{7,6},{9,8},{10,9},{11,10},{12... | collective-permute-start | bytes 196616 | tf_op jit(solution)/shard_map/while/body/eval_jaxpr/ppermute | solution.py:20
  871.4 400.8 %collective-permute-start = (f32[2,16,256]{2,1,0:T(8,128)}, f32[2,16,256]{2,1,0:T(8,128)}, u32[]{:S(2)}, u32[]{:S(2)}) collective-permute-start(f32[2,16,256]{2,1,0:T(8,128)} %slice_bitcast_fusion.7), channel_id=1, source_target_pairs={{8,0},{16,8},{24,16},{32,24},{40,32},{48,40},{56,48},{64,56},{72,6... | collective-permute-start | bytes 98312 | tf_op jit(solution)/shard_map/while/body/eval_jaxpr/ppermute | solution.py:20
  1186.7 82.1 %copy-start.12 = (f32[32]{0:T(128)S(1)}, f32[32]{0:T(128)}, u32[]{:S(2)}) copy-start(f32[32]{0:T(128)} %get-tuple-element.438) | copy-start | bytes 388 | tf_op jit(solution)/shard_map/while
  1186.7 82.1 %copy-start.16 = (f32[32]{0:T(128)S(1)}, f32[32]{0:T(128)}, u32[]{:S(2)}) copy-start(f32[32]{0:T(128)} %get-tuple-element.466) | copy-start | bytes 388 | tf_op jit(solution)/shard_map/while
  1186.7 82.1 %copy-start.17 = (f32[32]{0:T(128)S(1)}, f32[32]{0:T(128)}, u32[]{:S(2)}) copy-start(f32[32]{0:T(128)} %get-tuple-element.467) | copy-start | bytes 388 | tf_op jit(solution)/shard_map/while
  1186.7 82.7 %copy-start.9 = (s32[32]{0:T(128)S(1)}, s32[32]{0:T(128)}, u32[]{:S(2)}) copy-start(s32[32]{0:T(128)} %get-tuple-element.409) | copy-start | bytes 388 | tf_op jit(solution)/shard_map/while
  1274.2 9.8 collective-permute-start.3
  1276.3 7.9 collective-permute-start.2
  1292.1 316.1 %copy-start.20 = (s32[32]{0:T(128)}, s32[32]{0:T(128)S(1)}, u32[]{:S(2)}) copy-start(s32[32]{0:T(128)S(1)} %get-tuple-element.465) | copy-start | bytes 388 | tf_op jit(solution)/shard_map/while
  1293.7 401.1 %collective-permute-start.1 = (f32[2,32,256]{2,1,0:T(8,128)}, f32[2,32,256]{2,1,0:T(8,128)}, u32[]{:S(2)}, u32[]{:S(2)}) collective-permute-start(f32[2,32,256]{2,1,0:T(8,128)} %pad_maximum_fusion.10), channel_id=1, source_target_pairs={{1,0},{2,1},{3,2},{4,3},{5,4},{6,5},{7,6},{9,8},{10,9},{11,10},{12... | collective-permute-start | bytes 196616 | tf_op jit(solution)/shard_map/while/body/eval_jaxpr/ppermute | solution.py:20
  1296.2 400.8 %collective-permute-start = (f32[2,16,256]{2,1,0:T(8,128)}, f32[2,16,256]{2,1,0:T(8,128)}, u32[]{:S(2)}, u32[]{:S(2)}) collective-permute-start(f32[2,16,256]{2,1,0:T(8,128)} %slice_bitcast_fusion.7), channel_id=1, source_target_pairs={{8,0},{16,8},{24,16},{32,24},{40,32},{48,40},{56,48},{64,56},{72,6... | collective-permute-start | bytes 98312 | tf_op jit(solution)/shard_map/while/body/eval_jaxpr/ppermute | solution.py:20
  1611.5 82.1 %copy-start.12 = (f32[32]{0:T(128)S(1)}, f32[32]{0:T(128)}, u32[]{:S(2)}) copy-start(f32[32]{0:T(128)} %get-tuple-element.438) | copy-start | bytes 388 | tf_op jit(solution)/shard_map/while
  1611.5 82.1 %copy-start.16 = (f32[32]{0:T(128)S(1)}, f32[32]{0:T(128)}, u32[]{:S(2)}) copy-start(f32[32]{0:T(128)} %get-tuple-element.466) | copy-start | bytes 388 | tf_op jit(solution)/shard_map/while
  1611.5 82.1 %copy-start.17 = (f32[32]{0:T(128)S(1)}, f32[32]{0:T(128)}, u32[]{:S(2)}) copy-start(f32[32]{0:T(128)} %get-tuple-element.467) | copy-start | bytes 388 | tf_op jit(solution)/shard_map/while
  1611.5 82.7 %copy-start.9 = (s32[32]{0:T(128)S(1)}, s32[32]{0:T(128)}, u32[]{:S(2)}) copy-start(s32[32]{0:T(128)} %get-tuple-element.409) | copy-start | bytes 388 | tf_op jit(solution)/shard_map/while
  1699.0 9.8 collective-permute-start.3
  1701.1 7.9 collective-permute-start.2
  1717.0 316.1 %copy-start.20 = (s32[32]{0:T(128)}, s32[32]{0:T(128)S(1)}, u32[]{:S(2)}) copy-start(s32[32]{0:T(128)S(1)} %get-tuple-element.465) | copy-start | bytes 388 | tf_op jit(solution)/shard_map/while
  1718.6 401.1 %collective-permute-start.1 = (f32[2,32,256]{2,1,0:T(8,128)}, f32[2,32,256]{2,1,0:T(8,128)}, u32[]{:S(2)}, u32[]{:S(2)}) collective-permute-start(f32[2,32,256]{2,1,0:T(8,128)} %pad_maximum_fusion.10), channel_id=1, source_target_pairs={{1,0},{2,1},{3,2},{4,3},{5,4},{6,5},{7,6},{9,8},{10,9},{11,10},{12... | collective-permute-start | bytes 196616 | tf_op jit(solution)/shard_map/while/body/eval_jaxpr/ppermute | solution.py:20
  1721.1 400.8 %collective-permute-start = (f32[2,16,256]{2,1,0:T(8,128)}, f32[2,16,256]{2,1,0:T(8,128)}, u32[]{:S(2)}, u32[]{:S(2)}) collective-permute-start(f32[2,16,256]{2,1,0:T(8,128)} %slice_bitcast_fusion.7), channel_id=1, source_target_pairs={{8,0},{16,8},{24,16},{32,24},{40,32},{48,40},{56,48},{64,56},{72,6... | collective-permute-start | bytes 98312 | tf_op jit(solution)/shard_map/while/body/eval_jaxpr/ppermute | solution.py:20
  2036.4 82.1 %copy-start.12 = (f32[32]{0:T(128)S(1)}, f32[32]{0:T(128)}, u32[]{:S(2)}) copy-start(f32[32]{0:T(128)} %get-tuple-element.438) | copy-start | bytes 388 | tf_op jit(solution)/shard_map/while
  2036.4 82.1 %copy-start.16 = (f32[32]{0:T(128)S(1)}, f32[32]{0:T(128)}, u32[]{:S(2)}) copy-start(f32[32]{0:T(128)} %get-tuple-element.466) | copy-start | bytes 388 | tf_op jit(solution)/shard_map/while
  2036.4 82.1 %copy-start.17 = (f32[32]{0:T(128)S(1)}, f32[32]{0:T(128)}, u32[]{:S(2)}) copy-start(f32[32]{0:T(128)} %get-tuple-element.467) | copy-start | bytes 388 | tf_op jit(solution)/shard_map/while
  2036.4 82.7 %copy-start.9 = (s32[32]{0:T(128)S(1)}, s32[32]{0:T(128)}, u32[]{:S(2)}) copy-start(s32[32]{0:T(128)} %get-tuple-element.409) | copy-start | bytes 388 | tf_op jit(solution)/shard_map/while
  2123.9 9.8 collective-permute-start.3
  2126.0 7.9 collective-permute-start.2
  (50 other events, 89.8 us)
where the time goes:
time: 2150 us; the launch traced here: 2140 us
  blocking collectives  1870 us (87%)
  local copies, waits for them, and re-layouts  95.4 us (4%)
  other arithmetic  80.4 us (4%)
  starting transfers between devices  37.6 us (2%)
  waiting for transfers between devices  30.2 us (1%)
  matrix products  27.2 us (1%)
    all_gather x5, blocking collectives, circuit_inputs(): lax.all_gather(volts, ('gz', 'gy'), axis=0, tiled=True)  1520 us
    while x5, blocking collectives  347 us
  transfers between devices with their start and end apart: 20, of which 5 were waited for; matrix products, arithmetic and copies ran while one was open for 6% of the time, Pallas kernels for 0%

commit v1 on v0

--- a/solution.py
+++ b/solution.py
@@ -99,7 +99,12 @@
 
     def circuit_inputs(volts, samples):
         volts_all, samples_all = (
-            lax.all_gather(volts, ("gz", "gy"), axis=0, tiled=True),
+            jnp.concatenate(
+                lax.all_to_all(
+                    jnp.stack([volts] * lax.axis_size(("gz", "gy"))), ("gz", "gy"), 0, 0
+                ),
+                axis=0,
+            ),
             lax.all_gather(samples, ("gz", "gy"), axis=0, tiled=True),
         )
         return whole_terms(

time: 2150 us -> 671 us (0.31)
  blocking collectives: 1870 us -> 329 us
  starting transfers between devices: 37.6 us -> 89.2 us
    all_gather x5 -> x0, blocking collectives: 1520 us -> none  [circuit_inputs(): lax.all_gather(volts, ('gz', 'gy'), axis=0, tiled=True)]
    all_to_all x0 -> x5, starting transfers between devices: none -> 49.8 us  [circuit_inputs(): lax.all_to_all(jnp.stack([volts] * lax.axis_size(('gz', 'gy'))), ('gz', '...]
  transfers between devices with their start and end apart: 20 -> 25, of which waited for: 5 -> 5; matrix products, arithmetic and copies ran while one was open for 6% -> 23% of each run, Pallas kernels for 0% -> 0%
where the time goes in v1:
time: 671 us; the launch traced here: 666 us
  blocking collectives  329 us (49%)
  local copies, waits for them, and re-layouts  104 us (15%)
  starting transfers between devices  89.2 us (13%)
  other arithmetic  86.1 us (13%)
  waiting for transfers between devices  28.4 us (4%)
  matrix products  26.5 us (4%)
    while x5, blocking collectives  329 us
    all_to_all x5, starting transfers between devices, circuit_inputs(): lax.all_to_all(jnp.stack([volts] * lax.axis_size(('gz', 'gy'))), ('gz', '...  49.8 us
    ppermute x20, starting transfers between devices, shifted(): lax.ppermute(value, axis, [(source, source + steps) for source in range(f...  39.4 us
    ppermute x20, waiting for transfers between devices, shifted(): lax.ppermute(value, axis, [(source, source + steps) for source in range(f...  28.3 us
    while x125, local copies, waits for them, and re-layouts  13.9 us
  transfers between devices with their start and end apart: 25, of which 5 were waited for; matrix products, arithmetic and copies ran while one was open for 23% of the time, Pallas kernels for 0%

profile of v1, /device:TPU:16, one launch (start us, length us, event | category | flops | bytes accessed | tf_op | source)
XLA Modules:
  0.0 666.0 jit_solution(5174719490487856245)
XLA Ops:
  5.8 1.6 gather_fusion.3
  7.4 2.1 copy.48
  9.5 1.6 gather_fusion.4
  11.7 652.6 %while.18 = (s32[]{:T(128)}, f32[3,32,16,256]{3,2,1,0:T(8,128)S(1)}, f32[3,32,16,256]{3,2,1,0:T(8,128)S(1)}, f32[128]{0:T(128)S(1)}, f32[32]{0:T(128)S(1)}, /*in...) while((s32[]{:T(128)}, ...), condition=%wide.region_2.0_spmd, body=%wide.region_0.0_spmd.sunk | while | flops 15647837 | bytes 67406304 | solution.py:134
  13.3 5.7 collective-permute-start.1
  21.6 8.8 %all-to-all-start = ((f32[128,1,128]{2,1,0:T(1,128)}), f32[128,1,128]{2,1,0:T(1,128)S(1)}, u32[]{:S(2)}, u32[]{:S(2)}) async-start(f32[128,1,128]{2,1,0:T(1,128)} %stack.32), calls=%async_computation | async-start | bytes 131072 | tf_op jit(solution)/shard_map/while/body/eval_jaxpr/all_to_all | solution.py:103
  35.3 1.9 broadcast_subtract_fusion.4
  40.3 1.4 dynamic-update-slice.2
  41.7 65.9 %all-reduce.4 = f32[4096]{0:T(1024)S(1)} all-reduce(f32[4096]{0:T(1024)} %dynamic-update-slice.2), channel_id=1, replica_groups=mesh['gz'=16,'gy'=8] {'gz','gy'}, use_global_device_ids=true, to_apply=%add.2 | all-reduce | flops 4096 | bytes 32768 | tf_op jit(solution)/shard_map/while
  113.8 1.5 gather_fusion.1
  126.7 2.5 collective-permute-start.3
  130.8 5.7 collective-permute-done.3
  142.6 1.5 pad_maximum_fusion.13
  145.7 1.9 collective-permute-start.1
  150.2 10.2 %all-to-all-start = ((f32[128,1,128]{2,1,0:T(1,128)}), f32[128,1,128]{2,1,0:T(1,128)S(1)}, u32[]{:S(2)}, u32[]{:S(2)}) async-start(f32[128,1,128]{2,1,0:T(1,128)} %stack.32), calls=%async_computation | async-start | bytes 131072 | tf_op jit(solution)/shard_map/while/body/eval_jaxpr/all_to_all | solution.py:103
  165.3 1.9 broadcast_subtract_fusion.4
  171.7 65.9 %all-reduce.4 = f32[4096]{0:T(1024)S(1)} all-reduce(f32[4096]{0:T(1024)} %dynamic-update-slice.2), channel_id=1, replica_groups=mesh['gz'=16,'gy'=8] {'gz','gy'}, use_global_device_ids=true, to_apply=%add.2 | all-reduce | flops 4096 | bytes 32768 | tf_op jit(solution)/shard_map/while
  243.8 1.5 gather_fusion.1
  256.8 2.5 collective-permute-start.3
  260.9 5.7 collective-permute-done.3
  272.6 1.5 pad_maximum_fusion.13
  275.8 1.9 collective-permute-start.1
  280.3 10.2 %all-to-all-start = ((f32[128,1,128]{2,1,0:T(1,128)}), f32[128,1,128]{2,1,0:T(1,128)S(1)}, u32[]{:S(2)}, u32[]{:S(2)}) async-start(f32[128,1,128]{2,1,0:T(1,128)} %stack.32), calls=%async_computation | async-start | bytes 131072 | tf_op jit(solution)/shard_map/while/body/eval_jaxpr/all_to_all | solution.py:103
  295.3 1.9 broadcast_subtract_fusion.4
  300.4 1.4 dynamic-update-slice.2
  301.8 65.9 %all-reduce.4 = f32[4096]{0:T(1024)S(1)} all-reduce(f32[4096]{0:T(1024)} %dynamic-update-slice.2), channel_id=1, replica_groups=mesh['gz'=16,'gy'=8] {'gz','gy'}, use_global_device_ids=true, to_apply=%add.2 | all-reduce | flops 4096 | bytes 32768 | tf_op jit(solution)/shard_map/while
  373.8 1.5 gather_fusion.1
  386.8 2.5 collective-permute-start.3
  390.9 5.7 collective-permute-done.3
  402.6 1.5 pad_maximum_fusion.13
  405.8 1.9 collective-permute-start.1
  410.3 10.2 %all-to-all-start = ((f32[128,1,128]{2,1,0:T(1,128)}), f32[128,1,128]{2,1,0:T(1,128)S(1)}, u32[]{:S(2)}, u32[]{:S(2)}) async-start(f32[128,1,128]{2,1,0:T(1,128)} %stack.32), calls=%async_computation | async-start | bytes 131072 | tf_op jit(solution)/shard_map/while/body/eval_jaxpr/all_to_all | solution.py:103
  425.4 1.9 broadcast_subtract_fusion.4
  430.4 1.4 dynamic-update-slice.2
  431.8 65.9 %all-reduce.4 = f32[4096]{0:T(1024)S(1)} all-reduce(f32[4096]{0:T(1024)} %dynamic-update-slice.2), channel_id=1, replica_groups=mesh['gz'=16,'gy'=8] {'gz','gy'}, use_global_device_ids=true, to_apply=%add.2 | all-reduce | flops 4096 | bytes 32768 | tf_op jit(solution)/shard_map/while
  503.9 1.5 gather_fusion.1
  516.8 2.5 collective-permute-start.3
  520.9 5.7 collective-permute-done.3
  532.7 1.5 pad_maximum_fusion.13
  535.9 1.9 collective-permute-start.1
  540.3 10.2 %all-to-all-start = ((f32[128,1,128]{2,1,0:T(1,128)}), f32[128,1,128]{2,1,0:T(1,128)S(1)}, u32[]{:S(2)}, u32[]{:S(2)}) async-start(f32[128,1,128]{2,1,0:T(1,128)} %stack.32), calls=%async_computation | async-start | bytes 131072 | tf_op jit(solution)/shard_map/while/body/eval_jaxpr/all_to_all | solution.py:103
  555.4 1.9 broadcast_subtract_fusion.4
  560.4 1.4 dynamic-update-slice.2
  561.8 65.9 %all-reduce.4 = f32[4096]{0:T(1024)S(1)} all-reduce(f32[4096]{0:T(1024)} %dynamic-update-slice.2), channel_id=1, replica_groups=mesh['gz'=16,'gy'=8] {'gz','gy'}, use_global_device_ids=true, to_apply=%add.2 | all-reduce | flops 4096 | bytes 32768 | tf_op jit(solution)/shard_map/while
  633.9 1.5 gather_fusion.1
  646.9 2.5 collective-permute-start.3
  651.0 5.7 collective-permute-done.3
  662.7 1.5 pad_maximum_fusion.13
  (452 shorter events, 194.7 us)
Async XLA Ops:
  2.0 3.8 copy-start.18
  4.7 7.0 %copy-start.2 = (f32[3,32,16,256]{3,2,1,0:T(8,128)S(1)}, f32[3,32,16,256]{3,2,1,0:T(8,128)}, u32[]{:S(2)}) copy-start(f32[3,32,16,256]{3,2,1,0:T(8,128)} %param.15) | copy-start | bytes 4718596
  4.7 7.0 %copy-start.7 = (f32[2,4,64,64]{3,2,1,0:T(8,128)S(1)}, f32[2,4,64,64]{3,2,1,0:T(8,128)}, u32[]{:S(2)}) copy-start(f32[2,4,64,64]{3,2,1,0:T(8,128)} %param.23) | copy-start | bytes 393220
  4.7 7.0 %copy-start.8 = (f32[2,64,64]{2,1,0:T(8,128)S(1)}, f32[2,64,64]{2,1,0:T(8,128)}, u32[]{:S(2)}) copy-start(f32[2,64,64]{2,1,0:T(8,128)} %param.21) | copy-start | bytes 98308
  4.7 7.0 %copy-start.12 = (s32[2,4]{1,0:T(2,128)S(1)}, s32[2,4]{1,0:T(2,128)}, u32[]{:S(2)}) copy-start(s32[2,4]{1,0:T(2,128)} %param.24) | copy-start | bytes 100
  4.8 7.0 %copy-start.16 = (f32[128]{0:T(128)S(1)}, f32[128]{0:T(128)}, u32[]{:S(2)}) copy-start(f32[128]{0:T(128)} %param.25) | copy-start | bytes 1540
  11.7 28.5 %copy-start.14 = (f32[32]{0:T(128)}, f32[32]{0:T(128)S(1)}, u32[]{:S(2)}) copy-start(f32[32]{0:T(128)S(1)} %get-tuple-element.438) | copy-start | bytes 388 | tf_op jit(solution)/shard_map/while
  13.3 109.0 %collective-permute-start.1 = (f32[2,32,256]{2,1,0:T(8,128)}, f32[2,32,256]{2,1,0:T(8,128)}, u32[]{:S(2)}, u32[]{:S(2)}) collective-permute-start(f32[2,32,256]{2,1,0:T(8,128)} %pad_maximum_fusion.10), channel_id=1, source_target_pairs={{1,0},{2,1},{3,2},{4,3},{5,4},{6,5},{7,6},{9,8},{10,9},{11,10},{12... | collective-permute-start | bytes 196616 | tf_op jit(solution)/shard_map/while/body/eval_jaxpr/ppermute | solution.py:20
  19.7 105.1 %collective-permute-start = (f32[2,16,256]{2,1,0:T(8,128)}, f32[2,16,256]{2,1,0:T(8,128)}, u32[]{:S(2)}, u32[]{:S(2)}) collective-permute-start(f32[2,16,256]{2,1,0:T(8,128)} %slice_bitcast_fusion.7), channel_id=1, source_target_pairs={{8,0},{16,8},{24,16},{32,24},{40,32},{48,40},{56,48},{64,56},{72,6... | collective-permute-start | bytes 98312 | tf_op jit(solution)/shard_map/while/body/eval_jaxpr/ppermute | solution.py:20
  21.6 90.0 %all-to-all-start = ((f32[128,1,128]{2,1,0:T(1,128)}), f32[128,1,128]{2,1,0:T(1,128)S(1)}, u32[]{:S(2)}, u32[]{:S(2)}) async-start(f32[128,1,128]{2,1,0:T(1,128)} %stack.32), calls=%async_computation | async-start | bytes 131072 | tf_op jit(solution)/shard_map/while/body/eval_jaxpr/all_to_all | solution.py:103
  108.3 13.3 %copy-start.17 = (f32[32]{0:T(128)S(1)}, f32[32]{0:T(128)}, u32[]{:S(2)}) copy-start(f32[32]{0:T(128)} %get-tuple-element.466) | copy-start | bytes 388 | tf_op jit(solution)/shard_map/while
  122.4 2.4 copy-start.4
  126.7 9.8 %collective-permute-start.3 = (f32[2,32,256]{2,1,0:T(8,128)S(1)}, f32[2,32,256]{2,1,0:T(8,128)S(1)}, u32[]{:S(2)}, u32[]{:S(2)}) collective-permute-start(f32[2,32,256]{2,1,0:T(8,128)S(1)} %pad_maximum_fusion.12), channel_id=1, source_target_pairs={{0,1},{1,2},{2,3},{3,4},{4,5},{5,6},{6,7},{8,9},{9,10},{10,11},{11... | collective-permute-start | bytes 196616 | tf_op jit(solution)/shard_map/while/body/eval_jaxpr/ppermute | solution.py:20
  129.4 7.3 %collective-permute-start.2 = (f32[2,16,256]{2,1,0:T(8,128)S(1)}, f32[2,16,256]{2,1,0:T(8,128)S(1)}, u32[]{:S(2)}, u32[]{:S(2)}) collective-permute-start(f32[2,16,256]{2,1,0:T(8,128)S(1)} %slice_bitcast_fusion.9), channel_id=1, source_target_pairs={{0,8},{8,16},{16,24},{24,32},{32,40},{40,48},{48,56},{56,64},{64,7... | collective-permute-start | bytes 98312 | tf_op jit(solution)/shard_map/while/body/eval_jaxpr/ppermute | solution.py:20
  144.2 26.2 %copy-start.14 = (f32[32]{0:T(128)}, f32[32]{0:T(128)S(1)}, u32[]{:S(2)}) copy-start(f32[32]{0:T(128)S(1)} %get-tuple-element.438) | copy-start | bytes 388 | tf_op jit(solution)/shard_map/while
  145.7 106.7 %collective-permute-start.1 = (f32[2,32,256]{2,1,0:T(8,128)}, f32[2,32,256]{2,1,0:T(8,128)}, u32[]{:S(2)}, u32[]{:S(2)}) collective-permute-start(f32[2,32,256]{2,1,0:T(8,128)} %pad_maximum_fusion.10), channel_id=1, source_target_pairs={{1,0},{2,1},{3,2},{4,3},{5,4},{6,5},{7,6},{9,8},{10,9},{11,10},{12... | collective-permute-start | bytes 196616 | tf_op jit(solution)/shard_map/while/body/eval_jaxpr/ppermute | solution.py:20
  148.3 106.5 %collective-permute-start = (f32[2,16,256]{2,1,0:T(8,128)}, f32[2,16,256]{2,1,0:T(8,128)}, u32[]{:S(2)}, u32[]{:S(2)}) collective-permute-start(f32[2,16,256]{2,1,0:T(8,128)} %slice_bitcast_fusion.7), channel_id=1, source_target_pairs={{8,0},{16,8},{24,16},{32,24},{40,32},{48,40},{56,48},{64,56},{72,6... | collective-permute-start | bytes 98312 | tf_op jit(solution)/shard_map/while/body/eval_jaxpr/ppermute | solution.py:20
  150.2 91.5 %all-to-all-start = ((f32[128,1,128]{2,1,0:T(1,128)}), f32[128,1,128]{2,1,0:T(1,128)S(1)}, u32[]{:S(2)}, u32[]{:S(2)}) async-start(f32[128,1,128]{2,1,0:T(1,128)} %stack.32), calls=%async_computation | async-start | bytes 131072 | tf_op jit(solution)/shard_map/while/body/eval_jaxpr/all_to_all | solution.py:103
  238.3 13.3 %copy-start.17 = (f32[32]{0:T(128)S(1)}, f32[32]{0:T(128)}, u32[]{:S(2)}) copy-start(f32[32]{0:T(128)} %get-tuple-element.466) | copy-start | bytes 388 | tf_op jit(solution)/shard_map/while
  252.4 2.4 copy-start.4
  256.8 9.8 %collective-permute-start.3 = (f32[2,32,256]{2,1,0:T(8,128)S(1)}, f32[2,32,256]{2,1,0:T(8,128)S(1)}, u32[]{:S(2)}, u32[]{:S(2)}) collective-permute-start(f32[2,32,256]{2,1,0:T(8,128)S(1)} %pad_maximum_fusion.12), channel_id=1, source_target_pairs={{0,1},{1,2},{2,3},{3,4},{4,5},{5,6},{6,7},{8,9},{9,10},{10,11},{11... | collective-permute-start | bytes 196616 | tf_op jit(solution)/shard_map/while/body/eval_jaxpr/ppermute | solution.py:20
  259.5 7.3 %collective-permute-start.2 = (f32[2,16,256]{2,1,0:T(8,128)S(1)}, f32[2,16,256]{2,1,0:T(8,128)S(1)}, u32[]{:S(2)}, u32[]{:S(2)}) collective-permute-start(f32[2,16,256]{2,1,0:T(8,128)S(1)} %slice_bitcast_fusion.9), channel_id=1, source_target_pairs={{0,8},{8,16},{16,24},{24,32},{32,40},{40,48},{48,56},{56,64},{64,7... | collective-permute-start | bytes 98312 | tf_op jit(solution)/shard_map/while/body/eval_jaxpr/ppermute | solution.py:20
  274.2 26.2 %copy-start.14 = (f32[32]{0:T(128)}, f32[32]{0:T(128)S(1)}, u32[]{:S(2)}) copy-start(f32[32]{0:T(128)S(1)} %get-tuple-element.438) | copy-start | bytes 388 | tf_op jit(solution)/shard_map/while
  275.8 106.7 %collective-permute-start.1 = (f32[2,32,256]{2,1,0:T(8,128)}, f32[2,32,256]{2,1,0:T(8,128)}, u32[]{:S(2)}, u32[]{:S(2)}) collective-permute-start(f32[2,32,256]{2,1,0:T(8,128)} %pad_maximum_fusion.10), channel_id=1, source_target_pairs={{1,0},{2,1},{3,2},{4,3},{5,4},{6,5},{7,6},{9,8},{10,9},{11,10},{12... | collective-permute-start | bytes 196616 | tf_op jit(solution)/shard_map/while/body/eval_jaxpr/ppermute | solution.py:20
  278.3 106.5 %collective-permute-start = (f32[2,16,256]{2,1,0:T(8,128)}, f32[2,16,256]{2,1,0:T(8,128)}, u32[]{:S(2)}, u32[]{:S(2)}) collective-permute-start(f32[2,16,256]{2,1,0:T(8,128)} %slice_bitcast_fusion.7), channel_id=1, source_target_pairs={{8,0},{16,8},{24,16},{32,24},{40,32},{48,40},{56,48},{64,56},{72,6... | collective-permute-start | bytes 98312 | tf_op jit(solution)/shard_map/while/body/eval_jaxpr/ppermute | solution.py:20
  280.3 91.5 %all-to-all-start = ((f32[128,1,128]{2,1,0:T(1,128)}), f32[128,1,128]{2,1,0:T(1,128)S(1)}, u32[]{:S(2)}, u32[]{:S(2)}) async-start(f32[128,1,128]{2,1,0:T(1,128)} %stack.32), calls=%async_computation | async-start | bytes 131072 | tf_op jit(solution)/shard_map/while/body/eval_jaxpr/all_to_all | solution.py:103
  368.4 13.3 %copy-start.17 = (f32[32]{0:T(128)S(1)}, f32[32]{0:T(128)}, u32[]{:S(2)}) copy-start(f32[32]{0:T(128)} %get-tuple-element.466) | copy-start | bytes 388 | tf_op jit(solution)/shard_map/while
  382.4 2.4 copy-start.3
  382.4 2.4 copy-start.4
  386.8 9.8 %collective-permute-start.3 = (f32[2,32,256]{2,1,0:T(8,128)S(1)}, f32[2,32,256]{2,1,0:T(8,128)S(1)}, u32[]{:S(2)}, u32[]{:S(2)}) collective-permute-start(f32[2,32,256]{2,1,0:T(8,128)S(1)} %pad_maximum_fusion.12), channel_id=1, source_target_pairs={{0,1},{1,2},{2,3},{3,4},{4,5},{5,6},{6,7},{8,9},{9,10},{10,11},{11... | collective-permute-start | bytes 196616 | tf_op jit(solution)/shard_map/while/body/eval_jaxpr/ppermute | solution.py:20
  389.5 7.3 %collective-permute-start.2 = (f32[2,16,256]{2,1,0:T(8,128)S(1)}, f32[2,16,256]{2,1,0:T(8,128)S(1)}, u32[]{:S(2)}, u32[]{:S(2)}) collective-permute-start(f32[2,16,256]{2,1,0:T(8,128)S(1)} %slice_bitcast_fusion.9), channel_id=1, source_target_pairs={{0,8},{8,16},{16,24},{24,32},{32,40},{40,48},{48,56},{56,64},{64,7... | collective-permute-start | bytes 98312 | tf_op jit(solution)/shard_map/while/body/eval_jaxpr/ppermute | solution.py:20
  404.2 26.2 %copy-start.14 = (f32[32]{0:T(128)}, f32[32]{0:T(128)S(1)}, u32[]{:S(2)}) copy-start(f32[32]{0:T(128)S(1)} %get-tuple-element.438) | copy-start | bytes 388 | tf_op jit(solution)/shard_map/while
  405.8 106.7 %collective-permute-start.1 = (f32[2,32,256]{2,1,0:T(8,128)}, f32[2,32,256]{2,1,0:T(8,128)}, u32[]{:S(2)}, u32[]{:S(2)}) collective-permute-start(f32[2,32,256]{2,1,0:T(8,128)} %pad_maximum_fusion.10), channel_id=1, source_target_pairs={{1,0},{2,1},{3,2},{4,3},{5,4},{6,5},{7,6},{9,8},{10,9},{11,10},{12... | collective-permute-start | bytes 196616 | tf_op jit(solution)/shard_map/while/body/eval_jaxpr/ppermute | solution.py:20
  408.4 106.5 %collective-permute-start = (f32[2,16,256]{2,1,0:T(8,128)}, f32[2,16,256]{2,1,0:T(8,128)}, u32[]{:S(2)}, u32[]{:S(2)}) collective-permute-start(f32[2,16,256]{2,1,0:T(8,128)} %slice_bitcast_fusion.7), channel_id=1, source_target_pairs={{8,0},{16,8},{24,16},{32,24},{40,32},{48,40},{56,48},{64,56},{72,6... | collective-permute-start | bytes 98312 | tf_op jit(solution)/shard_map/while/body/eval_jaxpr/ppermute | solution.py:20
  410.3 91.5 %all-to-all-start = ((f32[128,1,128]{2,1,0:T(1,128)}), f32[128,1,128]{2,1,0:T(1,128)S(1)}, u32[]{:S(2)}, u32[]{:S(2)}) async-start(f32[128,1,128]{2,1,0:T(1,128)} %stack.32), calls=%async_computation | async-start | bytes 131072 | tf_op jit(solution)/shard_map/while/body/eval_jaxpr/all_to_all | solution.py:103
  498.4 13.3 %copy-start.17 = (f32[32]{0:T(128)S(1)}, f32[32]{0:T(128)}, u32[]{:S(2)}) copy-start(f32[32]{0:T(128)} %get-tuple-element.466) | copy-start | bytes 388 | tf_op jit(solution)/shard_map/while
  512.5 2.4 copy-start.3
  512.5 2.4 copy-start.4
  516.8 9.8 %collective-permute-start.3 = (f32[2,32,256]{2,1,0:T(8,128)S(1)}, f32[2,32,256]{2,1,0:T(8,128)S(1)}, u32[]{:S(2)}, u32[]{:S(2)}) collective-permute-start(f32[2,32,256]{2,1,0:T(8,128)S(1)} %pad_maximum_fusion.12), channel_id=1, source_target_pairs={{0,1},{1,2},{2,3},{3,4},{4,5},{5,6},{6,7},{8,9},{9,10},{10,11},{11... | collective-permute-start | bytes 196616 | tf_op jit(solution)/shard_map/while/body/eval_jaxpr/ppermute | solution.py:20
  519.5 7.3 %collective-permute-start.2 = (f32[2,16,256]{2,1,0:T(8,128)S(1)}, f32[2,16,256]{2,1,0:T(8,128)S(1)}, u32[]{:S(2)}, u32[]{:S(2)}) collective-permute-start(f32[2,16,256]{2,1,0:T(8,128)S(1)} %slice_bitcast_fusion.9), channel_id=1, source_target_pairs={{0,8},{8,16},{16,24},{24,32},{32,40},{40,48},{48,56},{56,64},{64,7... | collective-permute-start | bytes 98312 | tf_op jit(solution)/shard_map/while/body/eval_jaxpr/ppermute | solution.py:20
  534.3 26.2 %copy-start.14 = (f32[32]{0:T(128)}, f32[32]{0:T(128)S(1)}, u32[]{:S(2)}) copy-start(f32[32]{0:T(128)S(1)} %get-tuple-element.438) | copy-start | bytes 388 | tf_op jit(solution)/shard_map/while
  535.9 106.7 %collective-permute-start.1 = (f32[2,32,256]{2,1,0:T(8,128)}, f32[2,32,256]{2,1,0:T(8,128)}, u32[]{:S(2)}, u32[]{:S(2)}) collective-permute-start(f32[2,32,256]{2,1,0:T(8,128)} %pad_maximum_fusion.10), channel_id=1, source_target_pairs={{1,0},{2,1},{3,2},{4,3},{5,4},{6,5},{7,6},{9,8},{10,9},{11,10},{12... | collective-permute-start | bytes 196616 | tf_op jit(solution)/shard_map/while/body/eval_jaxpr/ppermute | solution.py:20
  538.4 106.5 %collective-permute-start = (f32[2,16,256]{2,1,0:T(8,128)}, f32[2,16,256]{2,1,0:T(8,128)}, u32[]{:S(2)}, u32[]{:S(2)}) collective-permute-start(f32[2,16,256]{2,1,0:T(8,128)} %slice_bitcast_fusion.7), channel_id=1, source_target_pairs={{8,0},{16,8},{24,16},{32,24},{40,32},{48,40},{56,48},{64,56},{72,6... | collective-permute-start | bytes 98312 | tf_op jit(solution)/shard_map/while/body/eval_jaxpr/ppermute | solution.py:20
  540.3 91.5 %all-to-all-start = ((f32[128,1,128]{2,1,0:T(1,128)}), f32[128,1,128]{2,1,0:T(1,128)S(1)}, u32[]{:S(2)}, u32[]{:S(2)}) async-start(f32[128,1,128]{2,1,0:T(1,128)} %stack.32), calls=%async_computation | async-start | bytes 131072 | tf_op jit(solution)/shard_map/while/body/eval_jaxpr/all_to_all | solution.py:103
  628.4 13.3 %copy-start.17 = (f32[32]{0:T(128)S(1)}, f32[32]{0:T(128)}, u32[]{:S(2)}) copy-start(f32[32]{0:T(128)} %get-tuple-element.466) | copy-start | bytes 388 | tf_op jit(solution)/shard_map/while
  642.5 2.4 copy-start.4
  646.9 9.8 %collective-permute-start.3 = (f32[2,32,256]{2,1,0:T(8,128)S(1)}, f32[2,32,256]{2,1,0:T(8,128)S(1)}, u32[]{:S(2)}, u32[]{:S(2)}) collective-permute-start(f32[2,32,256]{2,1,0:T(8,128)S(1)} %pad_maximum_fusion.12), channel_id=1, source_target_pairs={{0,1},{1,2},{2,3},{3,4},{4,5},{5,6},{6,7},{8,9},{9,10},{10,11},{11... | collective-permute-start | bytes 196616 | tf_op jit(solution)/shard_map/while/body/eval_jaxpr/ppermute | solution.py:20
  649.6 7.3 %collective-permute-start.2 = (f32[2,16,256]{2,1,0:T(8,128)S(1)}, f32[2,16,256]{2,1,0:T(8,128)S(1)}, u32[]{:S(2)}, u32[]{:S(2)}) collective-permute-start(f32[2,16,256]{2,1,0:T(8,128)S(1)} %slice_bitcast_fusion.9), channel_id=1, source_target_pairs={{0,8},{8,16},{16,24},{24,32},{32,40},{40,48},{48,56},{56,64},{64,7... | collective-permute-start | bytes 98312 | tf_op jit(solution)/shard_map/while/body/eval_jaxpr/ppermute | solution.py:20
  (41 other events, 56.1 us)
